TPU v7x, 32 devices: a whole 2x2x4 slice. The times are simulated.
32 devices in a mesh: row: 4 (over x, core), col: 8 (over z, y).
Axes of the slice: x: 2, y: 2, z: 4, core: 2. Of those that a mesh axis runs over, the one named last changes fastest.
Arguments:
- p_valence: bfloat16 [4096, 4096], P('row', 'col'), as said below
- p_conduction: bfloat16 [4096, 4096], P('row', 'col'), as said below
- trial_vectors: bfloat16 [2, 4096, 4096], P(None, 'row', 'col'), may hold values from -6 to 6
- mask_valence: int32 [32, 32], replicated, may hold values from 0 to 1, as said below
- mask_conduction: int32 [32, 32], replicated, may hold values from 0 to 1, as said below
- mask_trial: int32 [32, 32], replicated, may hold values 0 or 1
- orbitals: bfloat16 [32, 128, 8192], P('row'), may hold values from -0.29882812 to 0.29882812
- sphere_starts: int32 [32], replicated, may hold values from 0 to 16, as said below
Outputs:
- kernel: bfloat16 [2, 4096, 4096], P(None, 'row', 'col')
- density: float32 [2, 16384], P(None, ('row', 'col'))
Inputs may be any that keep to these rules, and one draw needn't show every extreme that they name: `mask_valence`: symmetric, ones on the block diagonal and next to it. `mask_conduction`: symmetric, ones on the block diagonal and next to it. `p_valence`: symmetric. `p_conduction`: symmetric. `sphere_starts`: the first block's start is 0 and the last block's 32 - 16.
All inputs are finite; a program needn't handle non-finite values.
Results may differ from a plain program's by a relative error of at most 0.0049.
Values may be sent and summed in bfloat16 or wider, within the bound.
A program may use at most 320 MiB of HBM per device.

v0:
```python
import jax
import jax.numpy as jnp
from jax import lax
from jax.sharding import PartitionSpec as P

BS = 128
SPAN = 16
SP = 512


def broadcast(x, axis, root):
    mine = lax.axis_index(axis) == root
    return lax.psum(jnp.where(mine, x, jnp.zeros_like(x)), axis)


def masked(values, block_mask, row_index, col_index):
    leading_dims = values.shape[:-2]
    row_blocks = values.shape[-2] // BS
    col_blocks = values.shape[-1] // BS
    tile_mask = lax.dynamic_slice(
        block_mask, (row_index * row_blocks, col_index * col_blocks), (row_blocks, col_blocks)
    ).astype(values.dtype)
    shaped = values.reshape(leading_dims + (row_blocks, BS, col_blocks, BS))
    return (shaped * tile_mask[:, None, :, None]).reshape(values.shape)


def local(
    p_valence,
    p_conduction,
    trial_vectors,
    mask_valence,
    mask_conduction,
    mask_trial,
    orbitals,
    sphere_starts,
):
    row_index = lax.axis_index("row")
    col_index = lax.axis_index("col")
    valence = masked(p_valence, mask_valence, row_index, col_index)
    conduction = masked(p_conduction, mask_conduction, row_index, col_index)
    trials = masked(trial_vectors, mask_trial, row_index, col_index)
    vector_count = trials.shape[0]
    local_rows = trials.shape[1]
    local_cols = trials.shape[2]
    panels = lax.all_gather(trials, "col", axis=2, tiled=True)
    response = jnp.einsum(
        "vik,kj->vij",
        panels,
        lax.all_gather(conduction, "row", axis=0, tiled=True),
        preferred_element_type=jnp.float32,
    )
    response_half = response.astype(jnp.bfloat16)
    gathered = lax.all_gather(response_half, "row", axis=1, tiled=True)
    kernel_sum = jnp.einsum(
        "ik,vkj->vij",
        lax.all_gather(valence, "col", axis=1, tiled=True),
        gathered,
        preferred_element_type=jnp.float32,
    )
    kernel = masked(kernel_sum, mask_trial, row_index, col_index).astype(jnp.bfloat16)
    row_blocks = local_rows // BS
    col_blocks = local_cols // BS
    ratio = lax.axis_size("col") // lax.axis_size("row")
    own_part = lax.dynamic_slice_in_dim(orbitals, col_index % ratio * col_blocks, col_blocks, 0)
    partner = broadcast(own_part, "row", col_index // ratio)
    partner_padded = jnp.pad(
        partner.reshape(col_blocks, BS, SPAN, SP), ((0, 0), (0, 0), (SPAN, SPAN), (0, 0))
    )
    starts_rows = lax.dynamic_slice_in_dim(sphere_starts, row_index * row_blocks, row_blocks, 0)
    starts_cols = lax.dynamic_slice_in_dim(sphere_starts, col_index * col_blocks, col_blocks, 0)
    offsets = jnp.clip(starts_rows[:, None] - starts_cols[None, :] + SPAN, 0, 2 * SPAN)

    def take_frame(orbital_block, offset):
        return lax.dynamic_slice_in_dim(orbital_block, offset, SPAN, 1)

    def frames_for_row(offset_row):
        return jax.vmap(take_frame)(partner_padded, offset_row)

    frames = jax.vmap(frames_for_row)(offsets).reshape(row_blocks, col_blocks, BS, SPAN * SP)
    kernel_blocks = kernel.reshape(vector_count, row_blocks, BS, col_blocks, BS).transpose(
        0, 1, 3, 2, 4
    )
    applied = jnp.einsum(
        "vabmn,abnp->vamp", kernel_blocks, frames, preferred_element_type=jnp.float32
    )
    contrib = jnp.sum(orbitals[None] * applied, axis=2)
    slab_count = lax.axis_size("row") * lax.axis_size("col")
    density_grid = jnp.zeros((vector_count, slab_count, SP), jnp.float32)
    zero_index = jnp.zeros((), jnp.int32)
    for local_block in range(row_blocks):
        begin_slab = starts_rows[local_block]
        current = lax.dynamic_slice(
            density_grid, (zero_index, begin_slab, zero_index), (vector_count, SPAN, SP)
        )
        update = current + contrib[:, local_block].reshape(vector_count, SPAN, SP)
        density_grid = lax.dynamic_update_slice(
            density_grid, update, (zero_index, begin_slab, zero_index)
        )
    own_slab = lax.psum_scatter(density_grid, ("row", "col"), scatter_dimension=1, tiled=True)
    density = own_slab.reshape(vector_count, SP)
    return (kernel, density)


def solution(mesh):
    placed = (
        P("row", "col"),
        P("row", "col"),
        P(None, "row", "col"),
        P(),
        P(),
        P(),
        P("row", None, None),
        P(),
    )
    return jax.shard_map(
        local,
        mesh=mesh,
        in_specs=placed,
        out_specs=(P(None, "row", "col"), P(None, ("row", "col"))),
        check_vma=False,
    )
```

profile of v0, /device:TPU:0, one launch (start us, length us, event | category | flops | bytes accessed | tf_op | source)
XLA Modules:
  0.0 935.6 jit_solution(7683359424325019603)
XLA Ops:
  7.2 0.9 dynamic-slice_convert_fusion
  8.5 2.3 bitcast_multiply_fusion.3
  10.9 0.8 dynamic-slice_convert_fusion.2
  12.2 1.5 broadcast_multiply_fusion
  13.9 7.4 dynamic-slice_select_fusion
  21.2 11.8 %copy.28 = bf16[64,8,16,512]{3,2,1,0:T(8,128)(2,1)} copy(bf16[64,8,16,512]{3,1,2,0:T(8,128)(2,1)} %bitcast.123) | data formatting | bytes 16777216
  33.4 0.8 copy-done.2
  34.2 1.2 bitcast_multiply_fusion.2
  35.6 18.6 %convert_element_type.30 = f32[8,128,8192]{2,1,0:T(8,128)} convert(bf16[8,128,8192]{2,1,0:T(8,128)(2,1)} %param.14) | non-fusion elementwise | flops 8388608 | bytes 50331648 | tf_op jit(solution)/shard_map/convert_element_type | solution.py:86
  54.2 0.7 fusion.18
  65.0 213.2 %all-gather.5.cloned.1.call-done = bf16[2,1024,4096]{2,1,0:T(8,128)(2,1)} async-done(((bf16[2,1024,512]{2,1,0:T(8,128)(2,1)}), bf16[2,1024,4096]{2,1,0:T(8,128)(2,1)}) %all-gather.5.cloned.1.call-update) | async-done | bytes 16777232 | tf_op jit(solution)/shard_map/all_gather | solution.py:45
  278.2 14.5 %fusion.13 = bf16[2,1024,512]{2,1,0:T(8,128)(2,1)} fusion(bf16[2,1024,4096]{2,1,0:T(8,128)(2,1)} %all-gather.5.cloned.1.call-done, bf16[4096,512]{1,0:T(8,128)(2,1)} %all-gather.7.cloned.1.call-done), kind=kOutput, calls=%fused_computation.15 | convolution fusion | flops 8590983168 | bytes 23068672 | tf_op jit(solution)/shard_map/vik,kj->vij/dot_general | solution.py:46
  298.9 132.9 %all-reduce.5.cloned.1.call-done = bf16[4,128,16,512]{3,2,1,0:T(8,128)(2,1)} async-done(((bf16[4,128,16,512]{3,2,1,0:T(8,128)(2,1)}), bf16[4,128,16,512]{3,2,1,0:T(8,128)(2,1)}) %all-reduce.5.cloned.1.call-update) | async-done | bytes 8388624 | tf_op jit(solution)/shard_map/psum | solution.py:13
  431.8 12.1 %pad.4 = bf16[4,128,48,512]{3,2,1,0:T(8,128)(2,1)} pad(bf16[4,128,16,512]{3,2,1,0:T(8,128)(2,1)} %all-reduce.5.cloned.1.call-done, bf16[]{:T(256)} %constant.48.clone.1), padding=0_0x0_0x16_16x0_0 | pad | bytes 33554432 | tf_op jit(solution)/shard_map/jit(_pad)/pad | solution.py:66
  443.9 204.5 %while.1 = (s32[]{:T(128)}, bf16[4,128,48,512]{3,2,1,0:T(8,128)(2,1)}, s32[32,4]{0,1:T(4,128)S(1)}, bf16[32,128,16,512]{3,2,1,0:T(8,128)(2,1)}, s32[]{:T(128)}) while((s32[]{:T(128)}, bf16[4,128,48,512]{3,2,1,0:T(8,128)(2,1)}, s32[32,4]{0,1:T(4,128)S(1)}, bf16[32,128,16,512]{3,2,1,0:T(8,128)(2,1)}, s32[]{:T(128)}) %tuple.42), condition=%wide.while_cond, body=%wide.while_body.sunk | while | flops 2 | bytes 4195953 | solution.py:74
  444.6 5.7 dynamic-slice_dynamic-update-slice_fusion.2
  451.0 5.7 dynamic-slice_dynamic-update-slice_fusion.2
  456.7 0.6 fusion.22
  457.3 5.8 dynamic-slice_dynamic-update-slice_fusion.2
  463.7 5.7 dynamic-slice_dynamic-update-slice_fusion.2
  470.1 5.7 dynamic-slice_dynamic-update-slice_fusion.2
  475.9 0.6 fusion.22
  476.5 5.7 dynamic-slice_dynamic-update-slice_fusion.2
  482.9 5.7 dynamic-slice_dynamic-update-slice_fusion.2
  489.3 5.7 dynamic-slice_dynamic-update-slice_fusion.2
  495.7 5.7 dynamic-slice_dynamic-update-slice_fusion.2
  502.1 5.7 dynamic-slice_dynamic-update-slice_fusion.2
  507.8 0.6 fusion.22
  508.4 5.7 dynamic-slice_dynamic-update-slice_fusion.2
  514.2 0.6 fusion.22
  514.8 5.7 dynamic-slice_dynamic-update-slice_fusion.2
  521.2 5.7 dynamic-slice_dynamic-update-slice_fusion.2
  527.0 0.6 fusion.22
  527.6 5.7 dynamic-slice_dynamic-update-slice_fusion.2
  534.0 5.8 dynamic-slice_dynamic-update-slice_fusion.2
  540.4 5.7 dynamic-slice_dynamic-update-slice_fusion.2
  546.2 0.6 fusion.22
  546.7 5.7 dynamic-slice_dynamic-update-slice_fusion.2
  553.1 5.7 dynamic-slice_dynamic-update-slice_fusion.2
  559.5 5.7 dynamic-slice_dynamic-update-slice_fusion.2
  565.2 0.6 fusion.22
  565.8 6.2 dynamic-slice_dynamic-update-slice_fusion.2
  572.1 0.6 fusion.22
  572.7 5.7 dynamic-slice_dynamic-update-slice_fusion.2
  579.1 5.7 dynamic-slice_dynamic-update-slice_fusion.2
  585.4 5.7 dynamic-slice_dynamic-update-slice_fusion.2
  591.7 5.8 dynamic-slice_dynamic-update-slice_fusion.2
  598.2 5.7 dynamic-slice_dynamic-update-slice_fusion.2
  604.6 5.7 dynamic-slice_dynamic-update-slice_fusion.2
  611.0 5.7 dynamic-slice_dynamic-update-slice_fusion.2
  617.3 5.7 dynamic-slice_dynamic-update-slice_fusion.2
  623.7 5.7 dynamic-slice_dynamic-update-slice_fusion.2
  630.1 5.7 dynamic-slice_dynamic-update-slice_fusion.2
  636.4 5.7 dynamic-slice_dynamic-update-slice_fusion.2
  642.8 5.7 dynamic-slice_dynamic-update-slice_fusion.2
  648.4 98.3 %reshape.126 = bf16[8,4,128,8192,1]{3,2,1,0,4:T(8,128)(2,1)} reshape(bf16[32,128,16,512]{3,2,1,0:T(8,128)(2,1)} %get-tuple-element.9) | data formatting | bytes 134217728 | tf_op jit(solution)/shard_map/reshape | solution.py:79
  746.8 13.8 %fusion.7 = bf16[2,1024,512]{1,2,0:T(8,128)(2,1)S(1)} fusion(bf16[2,4096,512]{2,1,0:T(8,128)(2,1)} %all-gather.9.cloned.1.call-done, bf16[1024,4096]{1,0:T(8,128)(2,1)} %all-gather.11.cloned.1.call-done, f32[1024,512]{0,1:T(8,128)S(1)} %bitcast.131), kind=kOutput, calls=%fused_computation.10 | convolution fusion | flops 8592031744 | bytes 20971520 | tf_op jit(solution)/shard_map/ik,vkj->vij/dot_general | solution.py:54
  760.5 2.0 copy.29
  762.5 3.2 copy.18
  765.7 33.2 %fusion = f32[2,8,8192]{2,0,1:T(2,128)S(1)} fusion(f32[8,128,8192]{2,1,0:T(8,128)} %convert_element_type.30, bf16[8,4,128,8192,1]{3,2,1,0,4:T(8,128)(2,1)} %reshape.126, bf16[2,8,128,4,128]{4,2,3,0,1:T(8,128)(2,1)S(1)} %copy.18), kind=kOutput, calls=%fused_computation.3 | convolution fusion | flops 17213292544 | bytes 103284736 | tf_op jit(solution)/shard_map/vabmn,abnp->vamp/dot_general | solution.py:83
  801.9 0.7 copy.19
  802.7 3.9 copy.20
  806.6 120.9 %all-reduce.7.cloned.1.call-done = f32[2,32,512]{2,0,1:T(2,128)} async-done(((f32[2,32,512]{2,0,1:T(2,128)}), f32[2,32,512]{2,0,1:T(2,128)}) %all-reduce.7.cloned.1.call-update) | async-done | bytes 131088
  927.5 1.3 dynamic-slice_bitcast_fusion
  (111 shorter events, 22.3 us)
Async XLA Ops:
  7.2 5.1 copy-start.1
  7.2 57.8 %all-gather.7.cloned.1.call-start = ((), (), s32[]{:S(2)}) async-start(), calls=%async_computation.1 | async-start | bytes 5242880 | tf_op jit(solution)/shard_map/all_gather | solution.py:49
  10.9 267.3 %all-gather.5.cloned.1.call-start = ((), (), s32[]{:S(2)}) async-start(), calls=%async_computation | async-start | bytes 18874368 | tf_op jit(solution)/shard_map/all_gather | solution.py:45
  13.8 418.0 %all-reduce.5.cloned.1.call-start = ((), (), s32[]{:S(2)}) async-start(), calls=%async_computation.4 | async-start | bytes 16777216 | tf_op jit(solution)/shard_map/psum | solution.py:13
  33.0 1.2 copy-start.2
  33.0 2.5 copy-start.3
  33.0 713.7 %all-gather.11.cloned.1.call-start = ((), (), s32[]{:S(2)}) async-start(), calls=%async_computation.3 | async-start | bytes 9437184 | tf_op jit(solution)/shard_map/all_gather | solution.py:56
  35.4 711.3 %all-gather.9.cloned.1.call-start = ((), (), s32[]{:S(2)}) async-start(), calls=%async_computation.2 | async-start | bytes 10485760 | tf_op jit(solution)/shard_map/all_gather | solution.py:53
  292.8 634.7 %all-reduce.7.cloned.1.call-start = ((), (), s32[]{:S(2)}) async-start(), calls=%async_computation.5 | async-start | bytes 262144
  760.5 2.0 copy-start
Sparse Core Ops, SparseCore 0:
  11.0 37.2 all-gather.6
  50.9 227.2 all-gather.4
  280.7 151.0 all-reduce.4
  433.7 125.0 all-gather.10
  560.8 56.4 all-gather.8
  802.8 124.6 all-reduce.6
where the time goes:
time: 941 us; the launch traced here: 936 us
  waiting for transfers between devices  467 us (50%)
  local copies, waits for them, and re-layouts  344 us (37%)
  matrix products  61.5 us (7%)
  other arithmetic  32.9 us (3%)
  between operations  29.5 us (3%)
    all_gather x1, waiting for transfers between devices, local(): panels = lax.all_gather(trials, 'col', axis=2, tiled=True)  213 us
    gather x96, local copies, waits for them, and re-layouts  204 us
    psum x1, waiting for transfers between devices, broadcast(): return lax.psum(jnp.where(mine, x, jnp.zeros_like(x)), axis)  133 us
    unnamed x7, waiting for transfers between devices  121 us
    reshape x1, local copies, waits for them, and re-layouts, local(): jax.vmap(frames_for_row)(offsets)  98.3 us
    dot_general x1, matrix products, local(): jnp.einsum('vabmn,abnp->vamp', kernel_blocks, frames, preferred_element_t...  33.2 us
    unnamed x15, local copies, waits for them, and re-layouts  19.2 us
  transfers between devices with their start and end apart: 6, of which 3 were waited for; matrix products, arithmetic and copies ran while one was open for 40% of the time, Pallas kernels for 0%

commit v1 on v0

--- a/solution.py
+++ b/solution.py
@@ -42,7 +42,7 @@
     vector_count = trials.shape[0]
     local_rows = trials.shape[1]
     local_cols = trials.shape[2]
-    panels = lax.all_gather(trials, "col", axis=2, tiled=True)
+    panels = jnp.concatenate(lax.all_gather(trials, "col"), axis=2)
     response = jnp.einsum(
         "vik,kj->vij",
         panels,

time: 941 us -> 941 us (level)
  waiting for transfers between devices: 467 us -> 444 us
  local copies, waits for them, and re-layouts: 344 us -> 366 us
    all_gather x1, waiting for transfers between devices: 213 us -> 176 us  [local(): panels = jnp.concatenate(lax.all_gather(trials, 'col'), axis=2)]
    reshape x0 -> x1, local copies, waits for them, and re-layouts: none -> 21.9 us  [local(): panels = jnp.concatenate(lax.all_gather(trials, 'col'), axis=2)]
    all_gather x1, waiting for transfers between devices: 0.01 us -> 12.4 us  [local(): lax.all_gather(conduction, 'row', axis=0, tiled=True)]
  transfers between devices with their start and end apart: 6 -> 6, of which waited for: 3 -> 4; matrix products, arithmetic and copies ran while one was open for 40% -> 43% of each run, Pallas kernels for 0% -> 0%
where the time goes in v1:
time: 941 us; the launch traced here: 935 us
  waiting for transfers between devices  444 us (47%)
  local copies, waits for them, and re-layouts  366 us (39%)
  matrix products  61.6 us (7%)
  other arithmetic  33.1 us (4%)
  between operations  29.4 us (3%)
    gather x96, local copies, waits for them, and re-layouts  204 us
    all_gather x1, waiting for transfers between devices, local(): panels = jnp.concatenate(lax.all_gather(trials, 'col'), axis=2)  176 us
    psum x1, waiting for transfers between devices, broadcast(): return lax.psum(jnp.where(mine, x, jnp.zeros_like(x)), axis)  135 us
    unnamed x7, waiting for transfers between devices  121 us
    reshape x1, local copies, waits for them, and re-layouts, local(): jax.vmap(frames_for_row)(offsets)  98.3 us
    dot_general x1, matrix products, local(): jnp.einsum('vabmn,abnp->vamp', kernel_blocks, frames, preferred_element_t...  33.2 us
    reshape x1, local copies, waits for them, and re-layouts, local(): panels = jnp.concatenate(lax.all_gather(trials, 'col'), axis=2)  21.9 us
    unnamed x15, local copies, waits for them, and re-layouts  19.7 us
  transfers between devices with their start and end apart: 6, of which 4 were waited for; matrix products, arithmetic and copies ran while one was open for 43% of the time, Pallas kernels for 0%

profile of v1, /device:TPU:0, one launch (start us, length us, event | category | flops | bytes accessed | tf_op | source)
XLA Modules:
  0.0 935.4 jit_solution(14159790307048464209)
XLA Ops:
  7.2 0.8 dynamic-slice_convert_fusion.2
  8.6 3.1 broadcast_multiply_fusion
  11.8 0.8 dynamic-slice_convert_fusion
  12.9 1.1 bitcast_multiply_fusion.3
  14.2 7.2 dynamic-slice_select_fusion
  21.4 12.2 %copy.37 = bf16[64,8,16,512]{3,2,1,0:T(8,128)(2,1)} copy(bf16[64,8,16,512]{3,1,2,0:T(8,128)(2,1)} %bitcast.127) | data formatting | bytes 16777216
  34.0 0.8 copy-done.2
  34.8 1.2 bitcast_multiply_fusion.2
  36.2 18.6 %convert_element_type.30 = f32[8,128,8192]{2,1,0:T(8,128)} convert(bf16[8,128,8192]{2,1,0:T(8,128)(2,1)} %param.14) | non-fusion elementwise | flops 8388608 | bytes 50331648 | tf_op jit(solution)/shard_map/convert_element_type | solution.py:86
  54.8 0.7 fusion.18
  65.6 176.3 %all-gather.12.cloned.1.call-done = bf16[16,1024,512]{2,1,0:T(8,128)(2,1)} async-done(((bf16[2,1024,512]{2,1,0:T(8,128)(2,1)}), bf16[16,1024,512]{2,1,0:T(8,128)(2,1)}) %all-gather.12.cloned.1.call-update) | async-done | bytes 16777232 | tf_op jit(solution)/shard_map/all_gather | solution.py:45
  241.9 21.9 %copy.22 = bf16[2,1024,8,512]{1,3,2,0:T(8,128)(2,1)} copy(bf16[2,1024,8,512]{3,1,0,2:T(8,128)(2,1)} %bitcast.128) | data formatting | bytes 33554432 | tf_op jit(solution)/shard_map/reshape | solution.py:45
  263.8 12.4 %all-gather.6.cloned.1.call-done = bf16[4096,512]{1,0:T(8,128)(2,1)} async-done(((bf16[1024,512]{1,0:T(8,128)(2,1)}), bf16[4096,512]{1,0:T(8,128)(2,1)}) %all-gather.6.cloned.1.call-update) | async-done | bytes 4194320 | tf_op jit(solution)/shard_map/all_gather | solution.py:49
  276.1 14.6 %fusion.13 = bf16[2,1024,512]{2,1,0:T(8,128)(2,1)} fusion(bf16[2,1024,4096]{1,2,0:T(8,128)(2,1)} %bitcast.129, bf16[4096,512]{1,0:T(8,128)(2,1)} %all-gather.6.cloned.1.call-done), kind=kOutput, calls=%fused_computation.15 | convolution fusion | flops 8590983168 | bytes 23068672 | tf_op jit(solution)/shard_map/vik,kj->vij/dot_general | solution.py:46
  296.9 134.6 %all-reduce.5.cloned.1.call-done = bf16[4,128,16,512]{3,2,1,0:T(8,128)(2,1)} async-done(((bf16[4,128,16,512]{3,2,1,0:T(8,128)(2,1)}), bf16[4,128,16,512]{3,2,1,0:T(8,128)(2,1)}) %all-reduce.5.cloned.1.call-update) | async-done | bytes 8388624 | tf_op jit(solution)/shard_map/psum | solution.py:13
  431.5 12.1 %pad.4 = bf16[4,128,48,512]{3,2,1,0:T(8,128)(2,1)} pad(bf16[4,128,16,512]{3,2,1,0:T(8,128)(2,1)} %all-reduce.5.cloned.1.call-done, bf16[]{:T(256)} %constant.48.clone.1), padding=0_0x0_0x16_16x0_0 | pad | bytes 33554432 | tf_op jit(solution)/shard_map/jit(_pad)/pad | solution.py:66
  443.7 204.5 %while.1 = (s32[]{:T(128)}, bf16[4,128,48,512]{3,2,1,0:T(8,128)(2,1)}, s32[32,4]{0,1:T(4,128)S(1)}, bf16[32,128,16,512]{3,2,1,0:T(8,128)(2,1)}, s32[]{:T(128)}) while((s32[]{:T(128)}, bf16[4,128,48,512]{3,2,1,0:T(8,128)(2,1)}, s32[32,4]{0,1:T(4,128)S(1)}, bf16[32,128,16,512]{3,2,1,0:T(8,128)(2,1)}, s32[]{:T(128)}) %tuple.43), condition=%wide.while_cond, body=%wide.while_body.sunk | while | flops 2 | bytes 4195953 | solution.py:74
  443.7 0.6 fusion.22
  444.3 5.7 dynamic-slice_dynamic-update-slice_fusion.2
  450.1 0.6 fusion.22
  450.7 5.7 dynamic-slice_dynamic-update-slice_fusion.2
  457.0 5.8 dynamic-slice_dynamic-update-slice_fusion.2
  462.9 0.6 fusion.22
  463.5 5.7 dynamic-slice_dynamic-update-slice_fusion.2
  469.3 0.6 fusion.22
  469.9 5.7 dynamic-slice_dynamic-update-slice_fusion.2
  476.3 5.7 dynamic-slice_dynamic-update-slice_fusion.2
  482.0 0.6 fusion.22
  482.6 5.7 dynamic-slice_dynamic-update-slice_fusion.2
  488.5 0.6 fusion.22
  489.1 5.7 dynamic-slice_dynamic-update-slice_fusion.2
  495.4 5.7 dynamic-slice_dynamic-update-slice_fusion.2
  501.8 5.7 dynamic-slice_dynamic-update-slice_fusion.2
  508.2 5.7 dynamic-slice_dynamic-update-slice_fusion.2
  514.5 5.7 dynamic-slice_dynamic-update-slice_fusion.2
  521.0 5.7 dynamic-slice_dynamic-update-slice_fusion.2
  527.4 5.7 dynamic-slice_dynamic-update-slice_fusion.2
  533.7 5.8 dynamic-slice_dynamic-update-slice_fusion.2
  540.2 5.7 dynamic-slice_dynamic-update-slice_fusion.2
  546.5 5.7 dynamic-slice_dynamic-update-slice_fusion.2
  552.8 5.7 dynamic-slice_dynamic-update-slice_fusion.2
  559.2 5.7 dynamic-slice_dynamic-update-slice_fusion.2
  565.6 6.2 dynamic-slice_dynamic-update-slice_fusion.2
  572.4 5.7 dynamic-slice_dynamic-update-slice_fusion.2
  578.8 5.7 dynamic-slice_dynamic-update-slice_fusion.2
  585.1 5.7 dynamic-slice_dynamic-update-slice_fusion.2
  591.5 5.8 dynamic-slice_dynamic-update-slice_fusion.2
  597.9 5.7 dynamic-slice_dynamic-update-slice_fusion.2
  604.3 5.7 dynamic-slice_dynamic-update-slice_fusion.2
  610.7 5.7 dynamic-slice_dynamic-update-slice_fusion.2
  617.0 5.7 dynamic-slice_dynamic-update-slice_fusion.2
  623.4 5.7 dynamic-slice_dynamic-update-slice_fusion.2
  629.8 5.7 dynamic-slice_dynamic-update-slice_fusion.2
  636.1 5.7 dynamic-slice_dynamic-update-slice_fusion.2
  642.5 5.7 dynamic-slice_dynamic-update-slice_fusion.2
  648.2 98.3 %reshape.136 = bf16[8,4,128,8192,1]{3,2,1,0,4:T(8,128)(2,1)} reshape(bf16[32,128,16,512]{3,2,1,0:T(8,128)(2,1)} %get-tuple-element.9) | data formatting | bytes 134217728 | tf_op jit(solution)/shard_map/reshape | solution.py:79
  746.5 13.8 %fusion.7 = bf16[2,1024,512]{1,2,0:T(8,128)(2,1)S(1)} fusion(bf16[2,4096,512]{2,1,0:T(8,128)(2,1)} %all-gather.8.cloned.1.call-done, bf16[1024,4096]{1,0:T(8,128)(2,1)} %all-gather.10.cloned.1.call-done, f32[1024,512]{0,1:T(8,128)S(1)} %bitcast.137), kind=kOutput, calls=%fused_computation.10 | convolution fusion | flops 8592031744 | bytes 20971520 | tf_op jit(solution)/shard_map/ik,vkj->vij/dot_general | solution.py:54
  760.3 2.0 copy.38
  762.3 3.2 copy.26
  765.5 33.2 %fusion = f32[2,8,8192]{2,0,1:T(2,128)S(1)} fusion(f32[8,128,8192]{2,1,0:T(8,128)} %convert_element_type.30, bf16[8,4,128,8192,1]{3,2,1,0,4:T(8,128)(2,1)} %reshape.136, bf16[2,8,128,4,128]{4,2,3,0,1:T(8,128)(2,1)S(1)} %copy.26), kind=kOutput, calls=%fused_computation.3 | convolution fusion | flops 17213292544 | bytes 103284736 | tf_op jit(solution)/shard_map/vabmn,abnp->vamp/dot_general | solution.py:83
  801.6 0.7 copy.27
  802.4 3.9 copy.28
  806.4 120.9 %all-reduce.7.cloned.1.call-done = f32[2,32,512]{2,0,1:T(2,128)} async-done(((f32[2,32,512]{2,0,1:T(2,128)}), f32[2,32,512]{2,0,1:T(2,128)}) %all-reduce.7.cloned.1.call-update) | async-done | bytes 131088
  927.2 1.3 dynamic-slice_bitcast_fusion
  (112 shorter events, 23.4 us)
Async XLA Ops:
  7.2 5.8 copy-start.1
  7.2 234.7 %all-gather.12.cloned.1.call-start = ((), (), s32[]{:S(2)}) async-start(), calls=%async_computation.4 | async-start | bytes 18874368 | tf_op jit(solution)/shard_map/all_gather | solution.py:45
  11.8 264.4 %all-gather.6.cloned.1.call-start = ((), (), s32[]{:S(2)}) async-start(), calls=%async_computation | async-start | bytes 5242880 | tf_op jit(solution)/shard_map/all_gather | solution.py:49
  14.1 417.4 %all-reduce.5.cloned.1.call-start = ((), (), s32[]{:S(2)}) async-start(), calls=%async_computation.3 | async-start | bytes 16777216 | tf_op jit(solution)/shard_map/psum | solution.py:13
  33.6 1.2 copy-start.2
  33.6 2.5 copy-start.3
  33.6 712.9 %all-gather.10.cloned.1.call-start = ((), (), s32[]{:S(2)}) async-start(), calls=%async_computation.2 | async-start | bytes 9437184 | tf_op jit(solution)/shard_map/all_gather | solution.py:56
  36.0 710.5 %all-gather.8.cloned.1.call-start = ((), (), s32[]{:S(2)}) async-start(), calls=%async_computation.1 | async-start | bytes 10485760 | tf_op jit(solution)/shard_map/all_gather | solution.py:53
  290.8 636.5 %all-reduce.7.cloned.1.call-start = ((), (), s32[]{:S(2)}) async-start(), calls=%async_computation.5 | async-start | bytes 262144
  760.3 2.0 copy-start
Sparse Core Ops, SparseCore 0:
  11.9 229.9 all-gather.11
  243.5 32.6 all-gather.5
  278.6 152.8 all-reduce.4
  433.4 125.0 all-gather.9
  560.5 56.4 all-gather.7
  802.5 124.6 all-reduce.6
